TPU v7x, 32 devices: a whole 2x2x4 slice. The times are simulated.
32 devices in a mesh: prow: 2 (over y), pcol: 16 (over z, x, core).
Axes of the slice: x: 2, y: 2, z: 4, core: 2. Of those that a mesh axis runs over, the one named last changes fastest.
Arguments:
- matrix: float32 [32, 2, 256, 4, 16, 256], P(None, 'prow', None, None, 'pcol'), may hold values from -6 to 6
- inverses: float32 [3, 256, 256], replicated, as said below
Outputs:
- factored: float32 [32, 2, 256, 4, 16, 256], P(None, 'prow', None, None, 'pcol')
Inputs may be any that keep to these rules, and one draw needn't show every extreme that they name: Each of the 3 matrices of inverses is lower triangular with a positive diagonal.
All inputs are finite; a program needn't handle non-finite values.
Results may differ from a plain program's by a relative error of at most 0.0003.
Values sent between devices are 32-bit elements; how exact they have to be, the bound alone decides.
A program may use at most 256 MiB of HBM per device.

v0:
```python
import jax
import jax.numpy as jnp
from jax import lax
from jax.sharding import PartitionSpec as P

STEPS = 3


exact_precision = lax.Precision.HIGHEST


def broadcast(value, axis, source):
    kept = jnp.where(lax.axis_index(axis) == source, value, 0).astype(value.dtype)
    return lax.psum(kept, axis)


def apply_inverse(columns_in, inverse):
    return lax.dot_general(
        columns_in,
        inverse,
        (((1,), (1,)), ((), ())),
        precision=exact_precision,
        preferred_element_type=jnp.float32,
    )


def per_device(matrix, inverses):
    row_blocks = matrix.shape[0]
    panel_width = matrix.shape[2]
    col_blocks = matrix.shape[3]
    prow_size = lax.axis_size("prow")
    pcol_size = lax.axis_size("pcol")
    prow_index = lax.axis_index("prow")
    pcol_index = lax.axis_index("pcol")
    blocks_here = matrix.reshape(row_blocks * panel_width, col_blocks, panel_width)
    global_rows = (
        (jnp.arange(row_blocks, dtype=jnp.int32) * prow_size + prow_index)[:, None] * panel_width
        + jnp.arange(panel_width, dtype=jnp.int32)[None, :]
    ).reshape(-1)
    global_blocks = jnp.arange(col_blocks, dtype=jnp.int32) * pcol_size + pcol_index
    for factor_step in range(STEPS):
        owner_col = factor_step % pcol_size
        get_column = factor_step // pcol_size
        get_kept_mask = (global_rows >= factor_step * panel_width)[:, None]
        solved = jnp.where(
            get_kept_mask, apply_inverse(blocks_here[:, get_column, :], inverses[factor_step]), 0.0
        )
        rows_panel = broadcast(solved, "pcol", owner_col)
        pieces = []
        for block in range(col_blocks):
            target = block * pcol_size + pcol_index
            piece_rows = lax.dynamic_slice_in_dim(
                rows_panel, target // prow_size * panel_width, panel_width, 0
            )
            pieces.append(broadcast(piece_rows, "prow", target % prow_size))
        cols_panel = jnp.stack(pieces)
        columns = list(range(col_blocks))
        results = []
        for column in columns:
            product = lax.dot_general(
                rows_panel,
                cols_panel[column],
                (((1,), (1,)), ((), ())),
                precision=exact_precision,
                preferred_element_type=jnp.float32,
            )
            live_mask = (global_rows >= (factor_step + 1) * panel_width)[:, None] & (
                global_blocks[column] > factor_step
            )
            updated = jnp.where(
                live_mask, blocks_here[:, column, :] - product, blocks_here[:, column, :]
            )
            placed = (pcol_index == factor_step % pcol_size) & (column == factor_step // pcol_size)
            results.append(jnp.where(placed, rows_panel, updated))
        blocks_here = jnp.stack(results, axis=1)
    col_index = (
        global_blocks[:, None] * panel_width + jnp.arange(panel_width, dtype=jnp.int32)[None, :]
    )
    kept_mask = (global_rows[:, None, None] >= col_index[None]) | (global_blocks < STEPS)[
        None, :, None
    ]
    result = jnp.where(kept_mask, blocks_here, 0.0)
    return result.reshape(row_blocks, 1, panel_width, col_blocks, 1, panel_width)


def solution(mesh):
    in_specs = (P(None, "prow", None, None, "pcol", None), P())
    out_specs = P(None, "prow", None, None, "pcol", None)
    return jax.shard_map(
        per_device, mesh=mesh, in_specs=in_specs, out_specs=out_specs, check_vma=False
    )
```

profile of v0, /device:TPU:28, one launch (start us, length us, event | category | flops | bytes accessed | tf_op | source)
XLA Modules:
  0.0 1008.6 jit_solution(4055933570773882389)
XLA Ops:
  6.5 0.6 fusion.20
  9.4 0.1 fusion.19
  9.6 0.0 copy-start.3
  9.6 15.1 %copy.3 = f32[32,1,256,4,1,256]{5,2,0,3,4,1:T(8,128)S(1)} copy(f32[32,1,256,4,1,256]{5,4,3,2,1,0:T(1,128)} %param.2) | data formatting | bytes 67108864 | tf_op args[0]
  24.7 0.0 copy-start
  24.7 11.7 %copy-done = f32[32,1,256,4,1,256]{5,2,0,3,4,1:T(8,128)} copy-done((f32[32,1,256,4,1,256]{5,2,0,3,4,1:T(8,128)}, f32[32,1,256,4,1,256]{5,2,0,3,4,1:T(8,128)S(1)}, u32[]{:S(2)}) %copy-start) | copy-done | bytes 33554456
  36.3 10.3 %fusion.2 = f32[8192,256]{1,0:T(8,128)} fusion(f32[8192,4,256]{2,0,1:T(8,128)S(1)} %bitcast.69, pred[8192]{0:T(1024)(128)(4,1)S(1)} %ge.114, pred[]{:T(512)S(6)} %eq.47, f32[3,256,256]{2,1,0:T(8,128)S(1)} %copy-done.3), kind=kOutput, calls=%fused_computation.18 | convolution fusion | flops 6446645248 | bytes 17047552 | tf_op jit(solution)/shard_map/dot_general | solution.py:18
  46.6 0.0 all-reduce.8.cloned.1.call-update
  46.7 0.0 all-reduce.10.cloned.1.call-start
  46.8 169.8 %all-reduce.8.cloned.1.call-done = f32[8192,256]{1,0:T(8,128)} async-done(((f32[8192,256]{1,0:T(8,128)}), f32[8192,256]{1,0:T(8,128)}) %all-reduce.8.cloned.1.call-update) | async-done | bytes 8388624 | tf_op jit(solution)/shard_map/psum | solution.py:14
  216.6 2.2 dynamic-slice_select_fusion.8
  218.9 0.0 all-reduce.10.cloned.1.call-update
  218.9 0.0 all-reduce.12.cloned.1.call-start
  221.3 20.9 %all-reduce.10.cloned.1.call-done = f32[256,256]{1,0:T(8,128)} async-done(((f32[256,256]{1,0:T(8,128)}), f32[256,256]{1,0:T(8,128)}) %all-reduce.10.cloned.1.call-update) | async-done | bytes 262160 | tf_op jit(solution)/shard_map/psum | solution.py:14
  242.2 14.7 %fusion.5 = f32[8192,256]{1,0:T(8,128)S(1)} fusion(f32[8192,256]{1,0:T(8,128)} %all-reduce.8.cloned.1.call-done, f32[256,256]{1,0:T(8,128)} %all-reduce.10.cloned.1.call-done, f32[8192,4,256]{2,0,1:T(8,128)} %bitcast.70, pred[8192]{0:T(1024)(128)(4,1)S(1)} %get-tuple-element.34, pred[]{:T(512)S(6)} %eq.47), kind=kOutput, calls=%fused_computation.21 | convolution fusion | flops 6448742400 | bytes 33824768 | tf_op jit(solution)/shard_map/dot_general | solution.py:60
  256.9 3.3 copy-done.2
  260.2 10.3 %fusion.1 = f32[8192,256]{1,0:T(8,128)} fusion(f32[8192,256]{1,0:T(8,128)S(1)} %fusion.5, pred[8192]{0:T(1024)(128)(4,1)S(1)} %ge.111, pred[]{:T(512)S(6)} %eq.46, f32[3,256,256]{2,1,0:T(8,128)S(1)} %copy-done.3), kind=kOutput, calls=%fused_computation.16 | convolution fusion | flops 6446645248 | bytes 17047552 | tf_op jit(solution)/shard_map/dot_general | solution.py:18
  270.5 0.0 all-reduce.12.cloned.1.call-update
  270.5 0.0 all-reduce.14.cloned.1.call-start
  270.6 169.9 %all-reduce.12.cloned.1.call-done = f32[8192,256]{1,0:T(8,128)} async-done(((f32[8192,256]{1,0:T(8,128)}), f32[8192,256]{1,0:T(8,128)}) %all-reduce.12.cloned.1.call-update) | async-done | bytes 8388624 | tf_op jit(solution)/shard_map/psum | solution.py:14
  440.4 2.2 dynamic-slice_select_fusion.7
  442.7 0.0 all-reduce.14.cloned.1.call-update
  442.7 0.6 all-reduce.16.cloned.1.call-start
  445.6 20.4 %all-reduce.14.cloned.1.call-done = f32[256,256]{1,0:T(8,128)} async-done(((f32[256,256]{1,0:T(8,128)}), f32[256,256]{1,0:T(8,128)}) %all-reduce.14.cloned.1.call-update) | async-done | bytes 262160 | tf_op jit(solution)/shard_map/psum | solution.py:14
  466.0 14.7 %fusion.4 = f32[8192,256]{1,0:T(8,128)S(1)} fusion(f32[8192,256]{1,0:T(8,128)} %all-reduce.12.cloned.1.call-done, f32[8192,256]{1,0:T(8,128)} %copy-done.2, f32[256,256]{1,0:T(8,128)} %all-reduce.14.cloned.1.call-done, pred[8192]{0:T(1024)(128)(4,1)S(1)} %get-tuple-element.30, pred[]{:T(512)S(6)} %eq.46), kind=kOutput, calls=%fused_computation.20 | convolution fusion | flops 6448742400 | bytes 25436160 | tf_op jit(solution)/shard_map/dot_general | solution.py:60
  480.8 3.2 copy-done.1
  484.0 10.4 %fusion = f32[8192,256]{1,0:T(8,128)} fusion(f32[8192,256]{1,0:T(8,128)S(1)} %fusion.4, pred[8192]{0:T(1024)(128)(4,1)S(1)} %ge.109, pred[]{:T(512)S(6)} %eq.45, f32[3,256,256]{2,1,0:T(8,128)S(1)} %copy-done.3), kind=kOutput, calls=%fused_computation.14 | convolution fusion | flops 6446645248 | bytes 17047552 | tf_op jit(solution)/shard_map/dot_general | solution.py:18
  494.4 0.0 all-reduce.16.cloned.1.call-update
  494.4 0.2 all-reduce.18.cloned.1.call-start
  494.6 169.7 %all-reduce.16.cloned.1.call-done = f32[8192,256]{1,0:T(8,128)} async-done(((f32[8192,256]{1,0:T(8,128)}), f32[8192,256]{1,0:T(8,128)}) %all-reduce.16.cloned.1.call-update) | async-done | bytes 8388624 | tf_op jit(solution)/shard_map/psum | solution.py:14
  664.3 2.2 dynamic-slice_select_fusion.9
  666.5 0.0 all-reduce.18.cloned.1.call-update
  666.6 0.1 iota_add_fusion.1
  666.7 0.1 iota_add_fusion
  666.8 76.5 %all-reduce.18.cloned.1.call-done = (f32[256,256]{1,0:T(8,128)}, f32[256,256]{1,0:T(8,128)}, f32[256,256]{1,0:T(8,128)}, f32[256,256]{1,0:T(8,128)}, f32[256,256...) async-done(((f32[256,256]{1,0:T(8,128)}, f32[256,256]{1,0:T(8,128)}, ...) | async-done | bytes 2621456 | tf_op jit(solution)/shard_map/psum | solution.py:14
  743.3 14.7 %fusion.3 = f32[8192,256]{1,0:T(8,128)S(1)} fusion(f32[8192,256]{1,0:T(8,128)} %all-reduce.16.cloned.1.call-done, f32[8192,256]{1,0:T(8,128)} %copy-done.1, f32[256,256]{1,0:T(8,128)} %get-tuple-element.14, pred[8192]{0:T(1024)(128)(4,1)S(1)} %and.204, pred[]{:T(512)S(6)} %eq.45), kind=kOutput, calls=%fused_computation.19 | convolution fusion | flops 6448742400 | bytes 25436160 | tf_op jit(solution)/shard_map/dot_general | solution.py:60
  758.0 0.0 copy-start.12
  758.0 0.0 slice-start.2
  758.0 9.8 copy.4
  767.8 11.9 %subtract_select_fusion.8 = f32[8192,256]{1,0:T(8,128)S(1)} fusion(f32[8192,256]{1,0:T(8,128)} %all-reduce.8.cloned.1.call-done, f32[256,256]{1,0:T(8,128)S(1)} %copy-done.12, f32[8192,4,256]{2,0,1:T(8,128)} %bitcast.71, pred[8192]{0:T(1024)(128)(4,1)S(1)} %get-tuple-element.31), kind=kOutput, calls=%fused_computation.9 | convolution fusion | flops 6446645248 | bytes 25436160 | tf_op jit(solution)/shard_map/dot_general | solution.py:60
  779.7 0.0 slice-done.2
  779.8 0.0 slice-done.3
  779.8 0.0 copy-done.11
  779.8 0.0 copy-start.10
  779.8 0.0 slice-start
  779.8 10.7 %subtract_select_fusion.7 = f32[8192,256]{1,0:T(8,128)} fusion(f32[8192,256]{1,0:T(8,128)S(1)} %subtract_select_fusion.8, f32[8192,256]{1,0:T(8,128)S(1)} %bitcast.77, f32[256,256]{1,0:T(8,128)S(1)} %copy-done.11, pred[8192]{0:T(1024)(128)(4,1)S(1)} %get-tuple-element.27), kind=kOutput, calls=%fused_computation.8 | convolution fusion | flops 6446645248 | bytes 25436160 | tf_op jit(solution)/shard_map/dot_general | solution.py:60
  790.5 12.8 %subtract_select_fusion.6 = f32[8192,256]{1,0:T(8,128)} fusion(f32[8192,256]{1,0:T(8,128)} %subtract_select_fusion.7, f32[8192,256]{1,0:T(8,128)} %all-reduce.16.cloned.1.call-done, f32[256,256]{1,0:T(8,128)S(1)} %copy-done.10, pred[8192]{0:T(1024)(128)(4,1)S(1)} %and.207), kind=kOutput, calls=%fused_computation.7 | convolution fusion | flops 6446645248 | bytes 25436160 | tf_op jit(solution)/shard_map/dot_general | solution.py:60
  803.2 10.9 %copy.5 = f32[32,1,256,1,1,256]{5,4,3,2,1,0:T(1,128)} copy(f32[32,1,256,1,1,256]{5,2,0,4,3,1:T(8,128)} %bitcast.83) | data formatting | bytes 16777216 | tf_op jit(solution)/shard_map/stack | solution.py:75
  814.1 0.0 slice-done
  814.1 12.3 %subtract_select_fusion.5 = f32[8192,256]{1,0:T(8,128)} fusion(f32[8192,256]{1,0:T(8,128)S(1)} %bitcast.75, f32[256,256]{1,0:T(8,128)S(1)} %copy-done.9, f32[8192,4,256]{2,0,1:T(8,128)} %bitcast.72, pred[8192]{0:T(1024)(128)(4,1)S(1)} %get-tuple-element.33), kind=kOutput, calls=%fused_computation.6 | convolution fusion | flops 6446645248 | bytes 25436160 | tf_op jit(solution)/shard_map/dot_general | solution.py:60
  826.4 0.0 copy-done.8
  826.4 12.3 %subtract_select_fusion.4 = f32[8192,256]{1,0:T(8,128)} fusion(f32[8192,256]{1,0:T(8,128)} %subtract_select_fusion.5, f32[8192,256]{1,0:T(8,128)S(1)} %bitcast.77, f32[256,256]{1,0:T(8,128)S(1)} %copy-done.8, pred[8192]{0:T(1024)(128)(4,1)S(1)} %get-tuple-element.29), kind=kOutput, calls=%fused_computation.5 | convolution fusion | flops 6446645248 | bytes 25436160 | tf_op jit(solution)/shard_map/dot_general | solution.py:60
  838.7 12.4 %subtract_select_fusion.3 = f32[8192,256]{1,0:T(8,128)} fusion(f32[8192,256]{1,0:T(8,128)} %subtract_select_fusion.4, f32[8192,256]{1,0:T(8,128)} %all-reduce.16.cloned.1.call-done, f32[256,256]{1,0:T(8,128)S(1)} %copy-done.7, pred[8192]{0:T(1024)(128)(4,1)S(1)} %and.216), kind=kOutput, calls=%fused_computation.4 | convolution fusion | flops 6446645248 | bytes 25436160 | tf_op jit(solution)/shard_map/dot_general | solution.py:60
  851.1 11.1 %copy.6 = f32[32,1,256,1,1,256]{5,4,3,2,1,0:T(1,128)} copy(f32[32,1,256,1,1,256]{5,2,0,4,3,1:T(8,128)} %bitcast.84) | data formatting | bytes 16777216 | tf_op jit(solution)/shard_map/stack | solution.py:75
  862.3 0.0 copy-start.5
  862.3 0.0 slice-start.4
  862.3 12.4 %subtract_select_fusion.2 = f32[8192,256]{1,0:T(8,128)} fusion(f32[8192,256]{1,0:T(8,128)S(1)} %bitcast.75, f32[256,256]{1,0:T(8,128)S(1)} %copy-done.6, f32[8192,4,256]{2,0,1:T(8,128)} %bitcast.73, pred[8192]{0:T(1024)(128)(4,1)S(1)} %get-tuple-element.32), kind=kOutput, calls=%fused_computation.3 | convolution fusion | flops 6446645248 | bytes 25436160 | tf_op jit(solution)/shard_map/dot_general | solution.py:60
  874.7 0.0 copy-done.5
  874.7 0.0 slice-start.6
  874.7 12.4 %subtract_select_fusion.1 = f32[8192,256]{1,0:T(8,128)} fusion(f32[8192,256]{1,0:T(8,128)} %subtract_select_fusion.2, f32[8192,256]{1,0:T(8,128)S(1)} %bitcast.77, f32[256,256]{1,0:T(8,128)S(1)} %copy-done.5, pred[8192]{0:T(1024)(128)(4,1)S(1)} %get-tuple-element.28), kind=kOutput, calls=%fused_computation.2 | convolution fusion | flops 6446645248 | bytes 25436160 | tf_op jit(solution)/shard_map/dot_general | solution.py:60
  887.1 0.0 slice-start.7
  887.1 12.3 %subtract_select_fusion = f32[8192,256]{1,0:T(8,128)} fusion(f32[8192,256]{1,0:T(8,128)} %subtract_select_fusion.1, f32[8192,256]{1,0:T(8,128)S(1)} %bitcast.79, f32[256,256]{1,0:T(8,128)S(1)} %copy-done.4, pred[8192]{0:T(1024)(128)(4,1)S(1)} %and.225), kind=kOutput, calls=%fused_computation.1 | convolution fusion | flops 6446645248 | bytes 25436160 | tf_op jit(solution)/shard_map/dot_general | solution.py:60
  899.5 10.0 copy.7
  909.5 91.8 %or_select_fusion = f32[32,1,256,4,1,256]{5,4,3,2,1,0:T(1,128)} fusion(pred[4]{0:T(512)(128)(4,1)S(1)} %broadcast_compare_fusion, f32[32,1,256,1,1,256]{5,4,3,2,1,0:T(1,128)S(1)} %copy.7, f32[32,1,256,1,1,256]{5,4,3,2,1,0:T(1,128)} %copy.6, f32[32,1,256,1,1,256]{5,4,3,2,1,0:T(1,128)} %copy.5, f32[32,1,256,1,1,256]{5,4,3,2,1,0:T(1,128)S(1)} %bitcast.81, ...), kind=kLoop, calls=%fused_computation | loop fusion | flops 50331648 | bytes 67145728 | tf_op jit(solution)/shard_map/jit(_where)/select_n | solution.py:82
  (41 shorter events, 0.2 us)
Async XLA Ops:
  6.5 210.1 %all-reduce.8.cloned.1.call-start = ((), (), s32[]{:S(2)}) async-start(), calls=%async_computation | async-start | bytes 16777216 | tf_op jit(solution)/shard_map/psum | solution.py:14
  9.6 26.8 %copy-start.3 = (f32[3,256,256]{2,1,0:T(8,128)S(1)}, f32[3,256,256]{2,1,0:T(8,128)}, u32[]{:S(2)}) copy-start(f32[3,256,256]{2,1,0:T(8,128)} %param.3) | copy-start | bytes 2359300
  24.7 11.7 %copy-start = (f32[32,1,256,4,1,256]{5,2,0,3,4,1:T(8,128)}, f32[32,1,256,4,1,256]{5,2,0,3,4,1:T(8,128)S(1)}, u32[]{:S(2)}) copy-start(f32[32,1,256,4,1,256]{5,2,0,3,4,1:T(8,128)S(1)} %copy.3) | copy-start | bytes 100663296
  46.7 195.5 %all-reduce.10.cloned.1.call-start = ((), (), s32[]{:S(2)}) async-start(), calls=%async_computation.1 | async-start | bytes 524288 | tf_op jit(solution)/shard_map/psum | solution.py:14
  218.9 221.6 %all-reduce.12.cloned.1.call-start = ((), (), s32[]{:S(2)}) async-start(), calls=%async_computation.2 | async-start | bytes 16777216 | tf_op jit(solution)/shard_map/psum | solution.py:14
  256.9 3.3 copy-start.2
  270.5 195.5 %all-reduce.14.cloned.1.call-start = ((), (), s32[]{:S(2)}) async-start(), calls=%async_computation.3 | async-start | bytes 524288 | tf_op jit(solution)/shard_map/psum | solution.py:14
  442.7 221.7 %all-reduce.16.cloned.1.call-start = ((), (), s32[]{:S(2)}) async-start(), calls=%async_computation.4 | async-start | bytes 16777216 | tf_op jit(solution)/shard_map/psum | solution.py:14
  480.8 3.2 copy-start.1
  494.4 248.9 %all-reduce.18.cloned.1.call-start = ((), (), s32[]{:S(2)}) async-start(), calls=%async_computation.5 | async-start | bytes 5242880 | tf_op jit(solution)/shard_map/psum | solution.py:14
  758.0 9.9 copy-start.12
  758.0 21.8 %slice-start.2 = ((s8[8388608]{0:T(1024)(128)(4,1)}), s8[4194304]{0:T(1024)(128)(4,1)S(1)}, s32[]{:S(2)}) async-start(s8[8388608]{0:T(1024)(128)(4,1)} %bitcast.76), calls=%async_computation.8 | async-start | bytes 8388608
  767.8 11.9 %slice-start.3 = ((s8[8388608]{0:T(1024)(128)(4,1)}), s8[4194304]{0:T(1024)(128)(4,1)S(1)}, s32[]{:S(2)}) async-start(s8[8388608]{0:T(1024)(128)(4,1)} %bitcast.76), calls=%async_computation.9 | async-start | bytes 8388608
  767.8 11.9 %copy-start.11 = (f32[256,256]{1,0:T(8,128)S(1)}, f32[256,256]{1,0:T(8,128)}, u32[]{:S(2)}) copy-start(f32[256,256]{1,0:T(8,128)} %get-tuple-element.12) | copy-start | bytes 786436
  779.8 10.7 %copy-start.10 = (f32[256,256]{1,0:T(8,128)S(1)}, f32[256,256]{1,0:T(8,128)}, u32[]{:S(2)}) copy-start(f32[256,256]{1,0:T(8,128)} %get-tuple-element.13) | copy-start | bytes 786436
  779.8 34.3 %slice-start = ((s8[8388608]{0:T(1024)(128)(4,1)}), s8[4194304]{0:T(1024)(128)(4,1)S(1)}, s32[]{:S(2)}) async-start(s8[8388608]{0:T(1024)(128)(4,1)} %bitcast.74), calls=%async_computation.6 | async-start | bytes 8388608
  790.5 23.6 %slice-start.1 = ((s8[8388608]{0:T(1024)(128)(4,1)}), s8[4194304]{0:T(1024)(128)(4,1)S(1)}, s32[]{:S(2)}) async-start(s8[8388608]{0:T(1024)(128)(4,1)} %bitcast.74), calls=%async_computation.7 | async-start | bytes 8388608
  803.2 10.9 %copy-start.9 = (f32[256,256]{1,0:T(8,128)S(1)}, f32[256,256]{1,0:T(8,128)}, u32[]{:S(2)}) copy-start(f32[256,256]{1,0:T(8,128)} %get-tuple-element.8) | copy-start | bytes 786436
  814.1 12.3 %copy-start.8 = (f32[256,256]{1,0:T(8,128)S(1)}, f32[256,256]{1,0:T(8,128)}, u32[]{:S(2)}) copy-start(f32[256,256]{1,0:T(8,128)} %get-tuple-element.9) | copy-start | bytes 786436
  826.4 12.3 %copy-start.7 = (f32[256,256]{1,0:T(8,128)S(1)}, f32[256,256]{1,0:T(8,128)}, u32[]{:S(2)}) copy-start(f32[256,256]{1,0:T(8,128)} %get-tuple-element.10) | copy-start | bytes 786436
  851.1 11.1 %copy-start.6 = (f32[256,256]{1,0:T(8,128)S(1)}, f32[256,256]{1,0:T(8,128)}, u32[]{:S(2)}) copy-start(f32[256,256]{1,0:T(8,128)} %get-tuple-element.5) | copy-start | bytes 786436
  862.3 12.4 %copy-start.5 = (f32[256,256]{1,0:T(8,128)S(1)}, f32[256,256]{1,0:T(8,128)}, u32[]{:S(2)}) copy-start(f32[256,256]{1,0:T(8,128)} %get-tuple-element.6) | copy-start | bytes 786436
  862.3 24.8 %slice-start.4 = ((s8[8388608]{0:T(1024)(128)(4,1)}), s8[4194304]{0:T(1024)(128)(4,1)S(1)}, s32[]{:S(2)}) async-start(s8[8388608]{0:T(1024)(128)(4,1)} %bitcast.78), calls=%async_computation.10 | async-start | bytes 8388608
  874.7 12.4 %slice-start.5 = ((s8[8388608]{0:T(1024)(128)(4,1)}), s8[4194304]{0:T(1024)(128)(4,1)S(1)}, s32[]{:S(2)}) async-start(s8[8388608]{0:T(1024)(128)(4,1)} %bitcast.78), calls=%async_computation.11 | async-start | bytes 8388608
  874.7 12.4 %copy-start.4 = (f32[256,256]{1,0:T(8,128)S(1)}, f32[256,256]{1,0:T(8,128)}, u32[]{:S(2)}) copy-start(f32[256,256]{1,0:T(8,128)} %get-tuple-element.7) | copy-start | bytes 786436
  874.7 34.8 %slice-start.6 = ((s8[8388608]{0:T(1024)(128)(4,1)}), s8[4194304]{0:T(1024)(128)(4,1)S(1)}, s32[]{:S(2)}) async-start(s8[8388608]{0:T(1024)(128)(4,1)} %bitcast.80), calls=%async_computation.12 | async-start | bytes 8388608
  887.1 22.4 %slice-start.7 = ((s8[8388608]{0:T(1024)(128)(4,1)}), s8[4194304]{0:T(1024)(128)(4,1)S(1)}, s32[]{:S(2)}) async-start(s8[8388608]{0:T(1024)(128)(4,1)} %bitcast.80), calls=%async_computation.13 | async-start | bytes 8388608
Sparse Core Ops, SparseCore 0:
  46.8 169.7 all-reduce.7
  219.0 23.1 all-reduce.9
  270.6 169.7 all-reduce.11
  442.8 23.1 all-reduce.13
  494.5 169.7 all-reduce.15
  667.4 75.9 all-reduce.17
where the time goes:
time: 1020 us; the launch traced here: 1010 us
  waiting for transfers between devices  627 us (61%)
  matrix products  184 us (18%)
  other arithmetic  98.8 us (10%)
  local copies, waits for them, and re-layouts  75.8 us (7%)
  between operations  21.3 us (2%)
    psum x6, waiting for transfers between devices, broadcast(): return lax.psum(kept, axis)  627 us
    dot_general x12, matrix products, per_device(): lax.dot_general(rows_panel, cols_panel[column], (((1,), (1,)), ((), ())),...  153 us
    select_n x1, other arithmetic, per_device(): result = jnp.where(kept_mask, blocks_here, 0.0)  91.8 us
    another operation x4, local copies, waits for them, and re-layouts, per_device(): blocks_here = jnp.stack(results, axis=1)  41.8 us
    unnamed x43, local copies, waits for them, and re-layouts  33.3 us
    dot_general x3, matrix products, apply_inverse(): lax.dot_general(columns_in, inverse, (((1,), (1,)), ((), ())), precision=...  31 us
  transfers between devices with their start and end apart: 6, of which 6 were waited for; matrix products, arithmetic and copies ran while one was open for 0% of the time, Pallas kernels for 0%

commit v1 on v0

v1 whole, which is shorter than its diff:
```python
import functools

import jax
import jax.numpy as jnp
from jax import lax
from jax.experimental import pallas as pl
from jax.experimental.pallas import tpu as pltpu
from jax.sharding import PartitionSpec as P

STEPS = 3
WINDOW = 4
LAG = 2
MESH = pl.DeviceIdType.MESH
BF = jnp.bfloat16
F32 = jnp.float32


def split(value):
    high = value.astype(BF)
    return high, (value - high.astype(F32)).astype(BF)


def dot_nt(a, b):
    return lax.dot_general(a, b, (((1,), (1,)), ((), ())), preferred_element_type=F32)


def dot3(a, b):
    return dot_nt(a[0], b[0]) + (dot_nt(a[0], b[1]) + dot_nt(a[1], b[0]))


def kernel(
    n_prow, n_pcol, rb, cb, nb,
    a_hbm, src_hbm, inv_ref, out_hbm,
    panels, xch, abuf, obuf, cst, chi, clo, prow_f, prow_h,
    rsem, ssem, xrsem, xssem, asem, osem, lsem,
):
    p = lax.axis_index("prow")
    q = lax.axis_index("pcol")
    depth = n_pcol // 4
    z, x, c = q // 4, (q // 2) % 2, q % 2
    sib = q + 1 - 2 * c
    xn = q + 2 - 4 * x
    quarter = nb // 4
    lines = nb * cb * 2
    stride = cb * 2
    slots = 2 + cb

    barrier = pltpu.get_barrier_semaphore()

    def greet(pp, qq):
        pl.semaphore_signal(barrier, inc=1, device_id=(pp, qq), device_id_type=MESH)

    greet(p, sib)
    greet(p, xn)
    pl.when(z > 0)(lambda: greet(p, q - 4))
    pl.when(z < depth - 1)(lambda: greet(p, q + 4))
    for d in range(1, n_prow):
        greet((p + d) % n_prow, q)
    peers = 1 + n_prow + (z > 0).astype(jnp.int32) + (z < depth - 1).astype(jnp.int32)
    pl.semaphore_wait(barrier, peers)

    def cp_q(a, j, dev, si, ri):
        ref = panels.at[a, :, pl.ds(pl.multiple_of(j * quarter, quarter), quarter), :]
        return pltpu.make_async_remote_copy(
            src_ref=ref, dst_ref=ref, send_sem=ssem.at[a % WINDOW, si], recv_sem=rsem.at[a, ri],
            device_id=(p, dev), device_id_type=MESH,
        )

    def cp_k(a, k, dev, si):
        ref = panels.at[a, k]
        return pltpu.make_async_remote_copy(
            src_ref=ref, dst_ref=ref, send_sem=ssem.at[a % WINDOW, si], recv_sem=rsem.at[a, k],
            device_id=(p, dev), device_id_type=MESH,
        )

    mine = 2 * x + c
    other = 2 * (1 - x) + c
    send_z = lambda a: cp_q(a, mine, jnp.minimum(q + 4, n_pcol - 1), 0, 0)
    send_x = lambda a: cp_q(a, mine, xn, 1, 1)
    send_c1 = lambda a: cp_q(a, mine, sib, 2, 2)
    send_c2 = lambda a: cp_q(a, other, sib, 3, 3)
    recv_z = lambda a: cp_q(a, mine, sib, 0, 0)
    recv_x = lambda a: cp_q(a, other, sib, 1, 1)
    recv_c1 = lambda a: cp_q(a, 2 * x + 1 - c, sib, 2, 2)
    recv_c2 = lambda a: cp_q(a, 2 * (1 - x) + 1 - c, sib, 3, 3)

    def start(fn, a):
        @pl.when(a >= WINDOW)
        def _():
            fn(a - WINDOW).wait_send()
        fn(a).start()

    def drain(fn):
        for a in range(max(rb - WINDOW, 0), rb):
            fn(a).wait_send()

    def fwd_of(k):
        return k + 2 - 4 * ((k // 2) % 2)

    def block_of(s):
        return s + 1 if s < 2 else (s - 2) * n_pcol + q

    def cp_x(s, a, d):
        return pltpu.make_async_remote_copy(
            src_ref=panels.at[a], dst_ref=xch.at[s], send_sem=xssem.at[s, d], recv_sem=xrsem.at[s],
            device_id=((p + d) % n_prow, q), device_id_type=MESH,
        )

    def cp_l(s, a):
        return pltpu.make_async_copy(panels.at[a], xch.at[s], xrsem.at[s])

    def publish(a):
        for s in range(slots):
            g = block_of(s)

            @pl.when((g % n_prow == p) & (g // n_prow == a))
            def _():
                for d in range(1, n_prow):
                    cp_x(s, a, d).start()
                cp_l(s, a).start()

    def wait_slot(s):
        g = block_of(s)

        @pl.when(g % n_prow == p)
        def _():
            cp_l(s, 0).wait()

        @pl.when(g % n_prow != p)
        def _():
            cp_x(s, 0, 1).wait_recv()

    for k in range(STEPS):
        @pl.when(q == k)
        def _():
            copy = pltpu.make_async_copy(src_hbm, panels.at[:, k], lsem)
            copy.start()
            copy.wait()

    def a_in(a):
        return pltpu.make_async_copy(
            a_hbm.at[pl.ds(pl.multiple_of(a * lines, lines), lines), :], abuf.at[a % 2], asem.at[a % 2])

    def o_out(a):
        return pltpu.make_async_copy(
            obuf.at[a % 2], out_hbm.at[pl.ds(pl.multiple_of(a * lines, lines), lines), :], osem.at[a % 2])

    a_in(0).start()

    def const(i):
        return cst[0, i], cst[1, i]

    def solve(ref):
        p0 = dot3(split(ref[0]), const(0))
        s0 = split(p0)
        p1 = dot3(split(ref[1] - dot3(s0, const(3))), const(1))
        s1 = split(p1)
        p2 = dot3(split(ref[2] - dot3(s0, const(4)) - dot3(s1, const(5))), const(2))
        return p0, p1, p2

    def set_const(i, value):
        h, l = split(value)
        cst[0, i] = h
        cst[1, i] = l

    def compute(a):
        g = a * n_prow + p

        @pl.when(a + 1 < rb)
        def _():
            a_in(a + 1).start()

        @pl.when(a == 0)
        def _():
            wait_slot(0)
            wait_slot(1)
            for k in range(STEPS):
                set_const(k, inv_ref[k])
            set_const(3, dot3(split(xch[0, 0]), const(0)))
            set_const(4, dot3(split(xch[1, 0]), const(0)))
            set_const(5, dot3(split(xch[1, 1] - dot3(const(4), const(3))), const(1)))

        parts = solve(panels.at[a])
        for k in range(STEPS):
            v = jnp.where(g >= k, parts[k], 0.0)
            prow_f[k] = v
            h, l = split(v)
            prow_h[0, :, k * nb:(k + 1) * nb] = h
            prow_h[1, :, k * nb:(k + 1) * nb] = l

        for b in range(cb):
            gb = block_of(2 + b)
            first = jnp.minimum((gb - p + n_prow - 1) // n_prow, rb - 1)

            @pl.when(a == first)
            def _():
                wait_slot(2 + b)
                cols = solve(xch.at[2 + b])
                for k in range(STEPS):
                    h, l = split(cols[k])
                    chi[b, :, k * nb:(k + 1) * nb] = h
                    clo[b, :, k * nb:(k + 1) * nb] = l

        @pl.when(a >= 2)
        def _():
            o_out(a - 2).wait()
        a_in(a).wait()
        par = a % 2
        for b in range(cb):
            gb = block_of(2 + b)

            def put(value):
                for h in range(2):
                    obuf[par, pl.ds(b * 2 + h, nb, stride=stride), :] = value[:, h * 128:(h + 1) * 128]

            def updated():
                old = jnp.concatenate(
                    [abuf[par, pl.ds(b * 2 + h, nb, stride=stride), :] for h in range(2)], axis=1)
                return old - dot3((prow_h[0], prow_h[1]), (chi[b], clo[b]))

            @pl.when((gb >= STEPS) & (g > gb))
            def _():
                put(updated())

            @pl.when((gb >= STEPS) & (g == gb))
            def _():
                rows = lax.broadcasted_iota(jnp.int32, (nb, nb), 0)
                cols = lax.broadcasted_iota(jnp.int32, (nb, nb), 1)
                put(jnp.where(rows >= cols, updated(), 0.0))

            @pl.when((gb >= STEPS) & (g < gb))
            def _():
                put(jnp.zeros((nb, nb), F32))

            if b == 0:
                for k in range(STEPS):
                    @pl.when(gb == k)
                    def _():
                        put(prow_f[k])
        o_out(a).start()

    def step(t, carry):
        @pl.when(t < rb)
        def _():
            a = t

            @pl.when(z > 0)
            def _():
                recv_z(a).wait_recv()
                pl.when(z < depth - 1)(lambda: start(send_z, a))
                start(send_x, a)
                start(send_c1, a)

            for k in range(STEPS):
                @pl.when(q == k)
                def _():
                    start(lambda i: cp_k(i, k, xn, 1 + 2 * k), a)
                    start(lambda i: cp_k(i, k, sib, 2 + 2 * k), a)

        @pl.when((t >= 1) & (t < rb + 1))
        def _():
            a = t - 1

            @pl.when(z > 0)
            def _():
                recv_x(a).wait_recv()
                start(send_c2, a)

            for k in range(STEPS):
                @pl.when(q == fwd_of(k))
                def _():
                    cp_k(a, k, sib, 1 + 2 * k).wait_recv()
                    start(lambda i: cp_k(i, k, sib, 1 + 2 * k), a)

        @pl.when((t >= 2) & (t < rb + 2))
        def _():
            a = t - 2

            @pl.when(z > 0)
            def _():
                recv_c1(a).wait_recv()
                recv_c2(a).wait_recv()

            @pl.when(z == 0)
            def _():
                for k in range(STEPS):
                    @pl.when((q != k) & (q != fwd_of(k)))
                    def _():
                        cp_k(a, k, sib, 1 + 2 * k).wait_recv()
                if depth > 1:
                    start(send_z, a)

            publish(a)

        @pl.when(t >= 2 + LAG)
        def _():
            compute(t - 2 - LAG)

        return carry

    lax.fori_loop(0, rb + 2 + LAG, step, 0)

    pl.when(z < depth - 1)(lambda: drain(send_z))

    @pl.when(z > 0)
    def _():
        drain(send_x)
        drain(send_c1)
        drain(send_c2)

    for k in range(STEPS):
        @pl.when(q == k)
        def _():
            drain(lambda i: cp_k(i, k, xn, 1 + 2 * k))
            drain(lambda i: cp_k(i, k, sib, 2 + 2 * k))

        @pl.when(q == fwd_of(k))
        def _():
            drain(lambda i: cp_k(i, k, sib, 1 + 2 * k))
    for s in range(slots):
        @pl.when(block_of(s) % n_prow == p)
        def _():
            for d in range(1, n_prow):
                cp_x(s, 0, d).wait_send()
    for a in range(max(rb - 2, 0), rb):
        o_out(a).wait()


def per_device(n_prow, n_pcol, matrix, inverses):
    rb, _, nb, cb, _, _ = matrix.shape
    lines = matrix.reshape(rb * nb * cb * 2, nb // 2)
    source = matrix[:, 0, :, 0, 0, :]
    vmem = pltpu.VMEM
    dma = pltpu.SemaphoreType.DMA
    out = pl.pallas_call(
        functools.partial(kernel, n_prow, n_pcol, rb, cb, nb),
        out_shape=jax.ShapeDtypeStruct(lines.shape, F32),
        in_specs=[
            pl.BlockSpec(memory_space=pl.ANY),
            pl.BlockSpec(memory_space=pl.ANY),
            pl.BlockSpec(memory_space=pltpu.VMEM),
        ],
        out_specs=pl.BlockSpec(memory_space=pl.ANY),
        scratch_shapes=[
            vmem((rb, STEPS, nb, nb), F32),
            vmem((2 + cb, STEPS, nb, nb), F32),
            vmem((2, nb * cb * 2, 128), F32),
            vmem((2, nb * cb * 2, 128), F32),
            vmem((2, 6, nb, nb), BF),
            vmem((cb, nb, STEPS * nb), BF),
            vmem((cb, nb, STEPS * nb), BF),
            vmem((STEPS, nb, nb), F32),
            vmem((2, nb, STEPS * nb), BF),
            dma((rb, 4)),
            dma((WINDOW, 8)),
            dma((2 + cb,)),
            dma((2 + cb, n_prow)),
            dma((2,)),
            dma((2,)),
            dma,
        ],
        compiler_params=pltpu.CompilerParams(
            collective_id=0, has_side_effects=True, vmem_limit_bytes=58 * 1024 * 1024
        ),
    )(lines, source, inverses)
    return out.reshape(matrix.shape)


def solution(mesh):
    in_specs = (P(None, "prow", None, None, "pcol", None), P())
    out_specs = P(None, "prow", None, None, "pcol", None)
    return jax.shard_map(
        functools.partial(per_device, mesh.shape["prow"], mesh.shape["pcol"]),
        mesh=mesh, in_specs=in_specs, out_specs=out_specs, check_vma=False,
    )
```

time: 1020 us -> 278 us (0.27); the launches traced: 1010 us -> 278 us
  waiting for transfers between devices: 627 us -> 0 us
  Pallas kernels: 0 us -> 240 us
  matrix products: 184 us -> 0 us
  other arithmetic: 98.8 us -> 0 us
  local copies, waits for them, and re-layouts: 75.8 us -> 38 us
  between operations: 21.3 us -> 0.02 us
    psum x6 -> x0, waiting for transfers between devices: 627 us -> none  [broadcast(): return lax.psum(kept, axis)]
    pallas_call x0 -> x1, Pallas kernels: none -> 240 us  [per_device(): pl.pallas_call(functools.partial(kernel, n_prow, n_pcol, rb, cb, nb), out...]
    dot_general x15 -> x0, matrix products: 184 us -> none  [the longest x12 153 us: per_device(): lax.dot_general(rows_panel, cols_panel[column], (((1,), (1,)), ((), ())),...]
    select_n x4 -> x0, other arithmetic: 98.5 us -> none  [the longest x1 91.8 us: per_device(): result = jnp.where(kept_mask, blocks_here, 0.0)]
    another operation x4 -> x0, local copies, waits for them, and re-layouts: 41.8 us -> none  [per_device(): blocks_here = jnp.stack(results, axis=1)]
    unnamed x43 -> x2, local copies, waits for them, and re-layouts: 33.3 us -> 30.9 us
  transfers between devices with their start and end apart: 6 -> 0, of which waited for: 6 -> 0; matrix products, arithmetic and copies ran while one was open for 0% -> 0% of each run, Pallas kernels for 0% -> 0%
where the time goes in v1:
time: 278 us
  Pallas kernels  240 us (86%)
  local copies, waits for them, and re-layouts  38 us (14%)
    pallas_call x1, Pallas kernels, per_device(): pl.pallas_call(functools.partial(kernel, n_prow, n_pcol, rb, cb, nb), out...  240 us
    unnamed x2, local copies, waits for them, and re-layouts  30.9 us
    slice x1, local copies, waits for them, and re-layouts, per_device(): source = matrix[:, 0, :, 0, 0, :]  7.13 us

profile of v1, /device:TPU:28, one launch (start us, length us, event | category | flops | bytes accessed | tf_op | source)
XLA Modules:
  0.0 278.1 jit_solution(14346679384646169040)
XLA Ops:
  0.0 7.1 %slice.3 = f32[32,1,256,1,1,256]{5,4,3,2,1,0:T(1,128)S(1)} slice(f32[32,1,256,4,1,256]{5,4,3,2,1,0:T(1,128)} %param.2), slice={[0:32], [0:1], [0:256], [0:1], [0:1], [0:256]} | slice | bytes 16777216 | tf_op jit(solution)/shard_map/slice | solution.py:332
  7.1 4.2 %copy.7 = f32[32,1,256,1,1,256]{5,2,0,4,3,1:T(8,128)} copy(f32[32,1,256,1,1,256]{5,4,3,2,1,0:T(1,128)S(1)} %slice.3) | data formatting | bytes 16777216
  11.3 240.1 %shard_map.28 = f32[65536,128]{1,0:T(8,128)} custom-call(f32[65536,128]{1,0:T(8,128)} %bitcast.6, f32[32,256,256]{2,1,0:T(8,128)} %bitcast.7, f32[3,256,256]{2,1,0:T(8,128)} %inv_ref.1), custom_call_target="tpu_custom_call" | custom-call | tf_op jit(solution)/shard_map/pallas_call | solution.py:335
  251.4 26.6 %copy.9 = f32[32,1,256,4,1,256]{5,4,3,2,1,0:T(1,128)} copy(f32[32,1,256,4,1,256]{5,4,3,2,1,0:T(1,128)} %bitcast.5) | data formatting | bytes 67108864

commit v2 on v1

--- a/solution.py
+++ b/solution.py
@@ -10,6 +10,7 @@
 STEPS = 3
 WINDOW = 4
 LAG = 2
+BACK = 3
 MESH = pl.DeviceIdType.MESH
 BF = jnp.bfloat16
 F32 = jnp.float32
@@ -30,9 +31,9 @@
 
 def kernel(
     n_prow, n_pcol, rb, cb, nb,
-    a_hbm, src_hbm, inv_ref, out_hbm,
-    panels, xch, abuf, obuf, cst, chi, clo, prow_f, prow_h,
-    rsem, ssem, xrsem, xssem, asem, osem, lsem,
+    a_hbm, inv_ref, out_hbm,
+    panels, xch, sbuf, abuf, obuf, cst, chi, clo, prow_f, prow_h,
+    rsem, ssem, xrsem, xssem, asem, osem, srcsem,
 ):
     p = lax.axis_index("prow")
     q = lax.axis_index("pcol")
@@ -84,6 +85,36 @@
     recv_c1 = lambda a: cp_q(a, 2 * x + 1 - c, sib, 2, 2)
     recv_c2 = lambda a: cp_q(a, 2 * (1 - x) + 1 - c, sib, 3, 3)
 
+    def cp_half(a, dev):
+        ref = panels.at[a, 0, pl.ds(nb // 2, nb // 2), :]
+        return pltpu.make_async_remote_copy(
+            src_ref=ref, dst_ref=ref, send_sem=ssem.at[a % WINDOW, 1], recv_sem=rsem.at[a, 0],
+            device_id=(p, dev), device_id_type=MESH,
+        )
+
+    def cp_dn(a, j, dev, si, ri):
+        ref = panels.at[a, 0, pl.ds(pl.multiple_of(j * quarter, quarter), quarter), :]
+        return pltpu.make_async_remote_copy(
+            src_ref=ref, dst_ref=ref, send_sem=ssem.at[a % WINDOW, si], recv_sem=rsem.at[a, ri],
+            device_id=(p, dev), device_id_type=MESH,
+        )
+
+    low = (z == 0) & (x == 1)
+    above = (z == 1) & (x == 1)
+    send_dn = lambda a: cp_dn(a, c, jnp.maximum(q - 4, 0), 4, 3)
+    recv_dn = lambda a: cp_dn(a, c, sib, 4, 3)
+    send_dc = lambda a: cp_dn(a, c, sib, 7, 4)
+    recv_dc = lambda a: cp_dn(a, 1 - c, sib, 7, 4)
+
+    def to_x(k):
+        return (lambda i: cp_half(i, xn)) if k == 0 else (lambda i: cp_k(i, k, xn, 1 + 2 * k))
+
+    def to_sib(k):
+        return lambda i: cp_k(i, k, sib, 2 + 2 * k)
+
+    def fwd(k):
+        return (lambda i: cp_half(i, sib)) if k == 0 else (lambda i: cp_k(i, k, sib, 1 + 2 * k))
+
     def start(fn, a):
         @pl.when(a >= WINDOW)
         def _():
@@ -130,13 +161,6 @@
         def _():
             cp_x(s, 0, 1).wait_recv()
 
-    for k in range(STEPS):
-        @pl.when(q == k)
-        def _():
-            copy = pltpu.make_async_copy(src_hbm, panels.at[:, k], lsem)
-            copy.start()
-            copy.wait()
-
     def a_in(a):
         return pltpu.make_async_copy(
             a_hbm.at[pl.ds(pl.multiple_of(a * lines, lines), lines), :], abuf.at[a % 2], asem.at[a % 2])
@@ -144,6 +168,14 @@
     def o_out(a):
         return pltpu.make_async_copy(
             obuf.at[a % 2], out_hbm.at[pl.ds(pl.multiple_of(a * lines, lines), lines), :], osem.at[a % 2])
+
+    def s_in(a):
+        return pltpu.make_async_copy(
+            a_hbm.at[pl.ds(pl.multiple_of(a * lines, lines), lines), :], sbuf.at[a % 2], srcsem.at[a % 2])
+
+    @pl.when(q < STEPS)
+    def _():
+        s_in(0).start()
 
     a_in(0).start()
 
@@ -254,8 +286,15 @@
             for k in range(STEPS):
                 @pl.when(q == k)
                 def _():
-                    start(lambda i: cp_k(i, k, xn, 1 + 2 * k), a)
-                    start(lambda i: cp_k(i, k, sib, 2 + 2 * k), a)
+                    s_in(a).wait()
+
+                    @pl.when(a + 1 < rb)
+                    def _():
+                        s_in(a + 1).start()
+                    for h in range(2):
+                        panels[a, k, :, h * 128:(h + 1) * 128] = sbuf[a % 2, pl.ds(h, nb, stride=stride), :]
+                    start(to_x(k), a)
+                    start(to_sib(k), a)
 
         @pl.when((t >= 1) & (t < rb + 1))
         def _():
@@ -265,12 +304,16 @@
             def _():
                 recv_x(a).wait_recv()
                 start(send_c2, a)
+
+            @pl.when(above)
+            def _():
+                start(send_dn, a)
 
             for k in range(STEPS):
                 @pl.when(q == fwd_of(k))
                 def _():
-                    cp_k(a, k, sib, 1 + 2 * k).wait_recv()
-                    start(lambda i: cp_k(i, k, sib, 1 + 2 * k), a)
+                    fwd(k)(a).wait_recv()
+                    start(fwd(k), a)
 
         @pl.when((t >= 2) & (t < rb + 2))
         def _():
@@ -284,21 +327,39 @@
             @pl.when(z == 0)
             def _():
                 for k in range(STEPS):
-                    @pl.when((q != k) & (q != fwd_of(k)))
+                    same = k + 1 - 2 * (k % 2)
+
+                    @pl.when(q == same)
                     def _():
                         cp_k(a, k, sib, 1 + 2 * k).wait_recv()
-                if depth > 1:
-                    start(send_z, a)
-
+
+                    @pl.when((q != k) & (q != same) & (q != fwd_of(k)))
+                    def _():
+                        fwd(k)(a).wait_recv()
+                start(send_z, a)
+
+            pl.when(jnp.logical_not(low))(lambda: publish(a))
+
+        @pl.when(low & (t >= 2 + BACK) & (t < rb + 2 + BACK))
+        def _():
+            a = t - 2 - BACK
+            recv_dn(a).wait_recv()
+            start(send_dc, a)
+
+        @pl.when(low & (t >= 3 + BACK) & (t < rb + 3 + BACK))
+        def _():
+            a = t - 3 - BACK
+            recv_dc(a).wait_recv()
             publish(a)
 
-        @pl.when(t >= 2 + LAG)
-        def _():
-            compute(t - 2 - LAG)
+        @pl.when((t >= 2 + lag) & (t < rb + 2 + lag))
+        def _():
+            compute(t - 2 - lag)
 
         return carry
 
-    lax.fori_loop(0, rb + 2 + LAG, step, 0)
+    lag = jnp.where(low, BACK + 1 + LAG, LAG)
+    lax.fori_loop(0, rb + 3 + BACK + LAG, step, 0)
 
     pl.when(z < depth - 1)(lambda: drain(send_z))
 
@@ -308,15 +369,18 @@
         drain(send_c1)
         drain(send_c2)
 
+    pl.when(above)(lambda: drain(send_dn))
+    pl.when(low)(lambda: drain(send_dc))
+
     for k in range(STEPS):
         @pl.when(q == k)
         def _():
-            drain(lambda i: cp_k(i, k, xn, 1 + 2 * k))
-            drain(lambda i: cp_k(i, k, sib, 2 + 2 * k))
+            drain(to_x(k))
+            drain(to_sib(k))
 
         @pl.when(q == fwd_of(k))
         def _():
-            drain(lambda i: cp_k(i, k, sib, 1 + 2 * k))
+            drain(fwd(k))
     for s in range(slots):
         @pl.when(block_of(s) % n_prow == p)
         def _():
@@ -329,14 +393,12 @@
 def per_device(n_prow, n_pcol, matrix, inverses):
     rb, _, nb, cb, _, _ = matrix.shape
     lines = matrix.reshape(rb * nb * cb * 2, nb // 2)
-    source = matrix[:, 0, :, 0, 0, :]
     vmem = pltpu.VMEM
     dma = pltpu.SemaphoreType.DMA
     out = pl.pallas_call(
         functools.partial(kernel, n_prow, n_pcol, rb, cb, nb),
         out_shape=jax.ShapeDtypeStruct(lines.shape, F32),
         in_specs=[
-            pl.BlockSpec(memory_space=pl.ANY),
             pl.BlockSpec(memory_space=pl.ANY),
             pl.BlockSpec(memory_space=pltpu.VMEM),
         ],
@@ -346,23 +408,24 @@
             vmem((2 + cb, STEPS, nb, nb), F32),
             vmem((2, nb * cb * 2, 128), F32),
             vmem((2, nb * cb * 2, 128), F32),
+            vmem((2, nb * cb * 2, 128), F32),
             vmem((2, 6, nb, nb), BF),
             vmem((cb, nb, STEPS * nb), BF),
             vmem((cb, nb, STEPS * nb), BF),
             vmem((STEPS, nb, nb), F32),
             vmem((2, nb, STEPS * nb), BF),
-            dma((rb, 4)),
+            dma((rb, 5)),
             dma((WINDOW, 8)),
             dma((2 + cb,)),
             dma((2 + cb, n_prow)),
             dma((2,)),
             dma((2,)),
-            dma,
+            dma((2,)),
         ],
         compiler_params=pltpu.CompilerParams(
             collective_id=0, has_side_effects=True, vmem_limit_bytes=58 * 1024 * 1024
         ),
-    )(lines, source, inverses)
+    )(lines, inverses)
     return out.reshape(matrix.shape)
 
 

time: 278 us -> 257 us (0.924)
  local copies, waits for them, and re-layouts: 38 us -> 26.6 us
  Pallas kernels: 240 us -> 230 us
    pallas_call x1, Pallas kernels: 240 us -> 230 us  [per_device(): pl.pallas_call(functools.partial(kernel, n_prow, n_pcol, rb, cb, nb), out...]
    slice x1 -> x0, local copies, waits for them, and re-layouts: 7.13 us -> none  [per_device(): source = matrix[:, 0, :, 0, 0, :]]
    unnamed x2 -> x1, local copies, waits for them, and re-layouts: 30.9 us -> 26.6 us
where the time goes in v2:
time: 257 us; the launch traced here: 256 us
  Pallas kernels  230 us (89%)
  local copies, waits for them, and re-layouts  26.6 us (10%)
    pallas_call x1, Pallas kernels, per_device(): pl.pallas_call(functools.partial(kernel, n_prow, n_pcol, rb, cb, nb), out...  230 us
    unnamed x1, local copies, waits for them, and re-layouts  26.6 us

profile of v2, /device:TPU:28, one launch (start us, length us, event | category | flops | bytes accessed | tf_op | source)
XLA Modules:
  0.0 256.4 jit_solution(5998042739949850706)
XLA Ops:
  0.0 229.7 %shard_map.28 = f32[65536,128]{1,0:T(8,128)} custom-call(f32[65536,128]{1,0:T(8,128)} %bitcast.3, f32[3,256,256]{2,1,0:T(8,128)} %inv_ref.1), custom_call_target="tpu_custom_call" | custom-call | tf_op jit(solution)/shard_map/pallas_call | solution.py:398
  229.8 26.6 %copy.5 = f32[32,1,256,4,1,256]{5,4,3,2,1,0:T(1,128)} copy(f32[32,1,256,4,1,256]{5,4,3,2,1,0:T(1,128)} %bitcast.2) | data formatting | bytes 67108864

commit v3 on v2

--- a/solution.py
+++ b/solution.py
@@ -8,7 +8,7 @@
 from jax.sharding import PartitionSpec as P
 
 STEPS = 3
-WINDOW = 4
+WINDOW = 8
 LAG = 2
 BACK = 3
 MESH = pl.DeviceIdType.MESH
@@ -21,18 +21,24 @@
     return high, (value - high.astype(F32)).astype(BF)
 
 
-def dot_nt(a, b):
-    return lax.dot_general(a, b, (((1,), (1,)), ((), ())), preferred_element_type=F32)
-
-
-def dot3(a, b):
-    return dot_nt(a[0], b[0]) + (dot_nt(a[0], b[1]) + dot_nt(a[1], b[0]))
+def left(value):
+    high, low = split(value)
+    return jnp.concatenate([high, high, low], axis=1)
+
+
+def right(value):
+    high, low = split(value)
+    return jnp.concatenate([high, low, high], axis=0)
+
+
+def dot(a, b):
+    return lax.dot_general(a, b, (((1,), (0,)), ((), ())), preferred_element_type=F32)
 
 
 def kernel(
     n_prow, n_pcol, rb, cb, nb,
     a_hbm, inv_ref, out_hbm,
-    panels, xch, sbuf, abuf, obuf, cst, chi, clo, prow_f, prow_h,
+    panels, xch, sbuf, abuf, obuf, cst, ccol, prow_f, prow_l,
     rsem, ssem, xrsem, xssem, asem, osem, srcsem,
 ):
     p = lax.axis_index("prow")
@@ -179,21 +185,9 @@
 
     a_in(0).start()
 
-    def const(i):
-        return cst[0, i], cst[1, i]
-
     def solve(ref):
-        p0 = dot3(split(ref[0]), const(0))
-        s0 = split(p0)
-        p1 = dot3(split(ref[1] - dot3(s0, const(3))), const(1))
-        s1 = split(p1)
-        p2 = dot3(split(ref[2] - dot3(s0, const(4)) - dot3(s1, const(5))), const(2))
-        return p0, p1, p2
-
-    def set_const(i, value):
-        h, l = split(value)
-        cst[0, i] = h
-        cst[1, i] = l
+        parts = jnp.concatenate([left(ref[0]), left(ref[1]), left(ref[2])], axis=1)
+        return tuple(dot(parts[:, :(k + 1) * 3 * nb], cst[k, :(k + 1) * 3 * nb, :]) for k in range(STEPS))
 
     def compute(a):
         g = a * n_prow + p
@@ -206,19 +200,25 @@
         def _():
             wait_slot(0)
             wait_slot(1)
-            for k in range(STEPS):
-                set_const(k, inv_ref[k])
-            set_const(3, dot3(split(xch[0, 0]), const(0)))
-            set_const(4, dot3(split(xch[1, 0]), const(0)))
-            set_const(5, dot3(split(xch[1, 1] - dot3(const(4), const(3))), const(1)))
+            def mul(u, v):
+                return dot(left(u), right(v))
+
+            r00, r11, r22 = inv_ref[0].T, inv_ref[1].T, inv_ref[2].T
+            w10 = mul(xch[0, 0], r00)
+            w20 = mul(xch[1, 0], r00)
+            r01 = -mul(mul(r00, w10.T), r11)
+            w21 = mul(xch[1, 0], r01) + mul(xch[1, 1], r11)
+            r02 = -mul(mul(r00, w20.T) + mul(r01, w21.T), r22)
+            r12 = -mul(mul(r11, w21.T), r22)
+            for k, column in enumerate(((r00,), (r01, r11), (r02, r12, r22))):
+                for m, value in enumerate(column):
+                    cst[k, m * 3 * nb:(m + 1) * 3 * nb, :] = right(value)
 
         parts = solve(panels.at[a])
         for k in range(STEPS):
             v = jnp.where(g >= k, parts[k], 0.0)
             prow_f[k] = v
-            h, l = split(v)
-            prow_h[0, :, k * nb:(k + 1) * nb] = h
-            prow_h[1, :, k * nb:(k + 1) * nb] = l
+            prow_l[:, k * 3 * nb:(k + 1) * 3 * nb] = left(v)
 
         for b in range(cb):
             gb = block_of(2 + b)
@@ -229,9 +229,7 @@
                 wait_slot(2 + b)
                 cols = solve(xch.at[2 + b])
                 for k in range(STEPS):
-                    h, l = split(cols[k])
-                    chi[b, :, k * nb:(k + 1) * nb] = h
-                    clo[b, :, k * nb:(k + 1) * nb] = l
+                    ccol[b, k * 3 * nb:(k + 1) * 3 * nb, :] = right(cols[k].T)
 
         @pl.when(a >= 2)
         def _():
@@ -248,7 +246,7 @@
             def updated():
                 old = jnp.concatenate(
                     [abuf[par, pl.ds(b * 2 + h, nb, stride=stride), :] for h in range(2)], axis=1)
-                return old - dot3((prow_h[0], prow_h[1]), (chi[b], clo[b]))
+                return old - dot(prow_l[...], ccol[b])
 
             @pl.when((gb >= STEPS) & (g > gb))
             def _():
@@ -409,11 +407,10 @@
             vmem((2, nb * cb * 2, 128), F32),
             vmem((2, nb * cb * 2, 128), F32),
             vmem((2, nb * cb * 2, 128), F32),
-            vmem((2, 6, nb, nb), BF),
-            vmem((cb, nb, STEPS * nb), BF),
-            vmem((cb, nb, STEPS * nb), BF),
+            vmem((STEPS, 3 * STEPS * nb, nb), BF),
+            vmem((cb, 3 * STEPS * nb, nb), BF),
             vmem((STEPS, nb, nb), F32),
-            vmem((2, nb, STEPS * nb), BF),
+            vmem((nb, 3 * STEPS * nb), BF),
             dma((rb, 5)),
             dma((WINDOW, 8)),
             dma((2 + cb,)),

time: 257 us -> 251 us (0.977)
  Pallas kernels: 230 us -> 224 us
    pallas_call x1, Pallas kernels: 230 us -> 224 us  [per_device(): pl.pallas_call(functools.partial(kernel, n_prow, n_pcol, rb, cb, nb), out...]
where the time goes in v3:
time: 251 us
  Pallas kernels  224 us (89%)
  local copies, waits for them, and re-layouts  26.6 us (11%)
    pallas_call x1, Pallas kernels, per_device(): pl.pallas_call(functools.partial(kernel, n_prow, n_pcol, rb, cb, nb), out...  224 us
    unnamed x1, local copies, waits for them, and re-layouts  26.6 us

profile of v3, /device:TPU:28, one launch (start us, length us, event | category | flops | bytes accessed | tf_op | source)
XLA Modules:
  0.0 251.1 jit_solution(5696081974643411475)
XLA Ops:
  0.0 224.5 %shard_map.28 = f32[65536,128]{1,0:T(8,128)} custom-call(f32[65536,128]{1,0:T(8,128)} %bitcast.3, f32[3,256,256]{2,1,0:T(8,128)} %inv_ref.1), custom_call_target="tpu_custom_call" | custom-call | tf_op jit(solution)/shard_map/pallas_call | solution.py:396
  224.5 26.6 %copy.5 = f32[32,1,256,4,1,256]{5,4,3,2,1,0:T(1,128)} copy(f32[32,1,256,4,1,256]{5,4,3,2,1,0:T(1,128)} %bitcast.2) | data formatting | bytes 67108864
